TPU v7x, 32 devices: a whole 2x2x4 slice. The times are simulated.
32 devices in a mesh: group: 2 (over x), chan: 16 (over z, y, core).
Axes of the slice: x: 2, y: 2, z: 4, core: 2. Of those that a mesh axis runs over, the one named last changes fastest.
Arguments:
- voltages: bfloat16 [32, 2, 256, 1024], P(('group', 'chan')), parts along dimension 0, may hold values from -6 to 6
- cal_num: float32 [32, 4, 512], P(('group', 'chan')), parts along dimension 0, may hold values from -6 to 6
- cal_weight: float32 [32, 2, 512], P(('group', 'chan')), parts along dimension 0, may hold values from 0.2 to 5
- flags: int32 [32, 512], P(('group', 'chan')), parts along dimension 0, may hold values 0 or 1
- positions: float32 [2, 512], replicated, may hold values from -300 to 300
- directions: float32 [2, 1024], replicated, may hold values from -0.05 to 0.05
- pointing: int32 [2048], P('group'), parts along dimension 0, may hold values from 0 to 1023, each once
Outputs:
- beam_power: bfloat16 [2048, 16, 128], P(('group', 'chan')), parts along dimension 0
- solved_gains: float32 [32, 4, 512], P(('group', 'chan')), parts along dimension 0
There are 2 independent parts, one for each index of `group`. A program takes and returns all parts, laid end to end along the dimension named above; an argument that names none is the same for every part. Nothing has to cross between parts.
Inputs may be any that keep to these rules, and one draw needn't show every extreme that they name: `pointing`: each table direction is named by exactly one beam.
All inputs are finite; a program needn't handle non-finite values. No bound on the sum of `flags` on one device may be relied on, other than what follows from the above.
Results may differ from a plain program's by a relative error of at most 0.004.
Values may be sent and summed in bfloat16 or wider, within the bound.
No kernel may reach another device: no remote copies, remote signals or barrier semaphores. Data moves between devices by JAX's collectives and lax.ppermute only.
A program may use at most 64 MiB of HBM per device.

v0:
```python
import jax
import jax.numpy as jnp
from jax import lax
from jax.sharding import PartitionSpec as P

ITERS = 8
PENALTY = 2.0
RIDGE = 1.0
TWO_PI = 6.283185307179586
HIGHEST = lax.Precision.HIGHEST


def basis_rows(channel_ids, total):
    place = 2.0 * (channel_ids.astype(jnp.float32) + 0.5) / total - 1.0
    return jnp.stack(
        [
            jnp.ones_like(place),
            place,
            0.5 * (3.0 * place * place - 1.0),
            0.5 * (5.0 * place * place * place - 3.0 * place),
        ],
        axis=1,
    )


def invert_small(matrix):
    order = matrix.shape[0]
    unit = jnp.ones_like(matrix[0, 0])
    nothing = jnp.zeros_like(matrix[0, 0])
    left = [[matrix[row, column] for column in range(order)] for row in range(order)]
    right = [
        [unit if row == column else nothing for column in range(order)] for row in range(order)
    ]
    for pivot in range(order):
        factor = 1.0 / left[pivot][pivot]
        left[pivot] = [entry * factor for entry in left[pivot]]
        right[pivot] = [entry * factor for entry in right[pivot]]
        for row in range(order):
            if row != pivot:
                scale = left[row][pivot]
                left[row] = [
                    first - scale * second for first, second in zip(left[row], left[pivot])
                ]
                right[row] = [
                    first - scale * second for first, second in zip(right[row], right[pivot])
                ]
    return jnp.stack([jnp.stack(line, 0) for line in right], 0)


def beam_matrices(fitted, usable, ratio, projected):
    phase = projected * (TWO_PI * ratio)
    cosine = jnp.cos(phase)
    sine = jnp.sin(phase)
    stations = projected.shape[1]
    scale = usable * stations ** (-0.5)
    matrices = []
    for polar in range(2):
        gain_re = (fitted[2 * polar] * scale)[None, :]
        gain_im = (fitted[2 * polar + 1] * scale)[None, :]
        w_re = (gain_re * cosine - gain_im * sine).astype(jnp.bfloat16)
        w_im = (-(gain_re * sine + gain_im * cosine)).astype(jnp.bfloat16)
        upper = jnp.concatenate([w_re, -w_im], axis=1)
        lower = jnp.concatenate([w_im, w_re], axis=1)
        matrices.append(jnp.concatenate([upper, lower], axis=0))
    return matrices


def detect(matrices, volts):
    beams = matrices[0].shape[0] // 2
    total = jnp.zeros((beams, volts.shape[1]), jnp.float32)
    for polar in range(2):
        output = lax.dot_general(
            matrices[polar],
            volts[polar],
            (((1,), (1,)), ((), ())),
            preferred_element_type=jnp.float32,
        )
        total = total + output[:beams] * output[:beams] + output[beams:] * output[beams:]
    return total


def average_pairs(power):
    return ((power[..., 0::2] + power[..., 1::2]) * 0.5).astype(jnp.bfloat16)


def body(voltages, cal_num, cal_weight, flags, positions, directions, pointing):
    local_count = voltages.shape[0]
    devices = lax.axis_size("chan")
    total = local_count * devices
    channel_ids = lax.axis_index("chan") * local_count + jnp.arange(local_count, dtype=jnp.int32)
    basis = basis_rows(channel_ids, total)
    usable = flags.astype(jnp.float32)
    gram = jnp.einsum("ck,cj,cs->kjs", basis, basis, usable, precision=HIGHEST)
    order = basis.shape[1]
    identity = jnp.eye(order, dtype=jnp.float32)[:, :, None]
    weight4 = jnp.repeat(cal_weight, 2, axis=1)
    mask = usable[:, None, :]
    fitted = jnp.zeros(cal_num.shape, jnp.float32)
    dual = jnp.zeros(cal_num.shape, jnp.float32)
    inverse = None
    for sweep in range(ITERS):
        local = (mask * cal_num + PENALTY * (fitted - dual)) / (mask * weight4 + PENALTY)
        numerator = jnp.einsum("ck,cqs->kqs", basis, mask * (local + dual), precision=HIGHEST)
        if sweep == 0:
            gram_all, summed = lax.psum((gram, numerator), "chan")
            inverse = invert_small(gram_all + RIDGE * identity)
        else:
            summed = lax.psum(numerator, "chan")
        coefficients = jnp.einsum("kjs,jqs->kqs", inverse, summed, precision=HIGHEST)
        fitted = jnp.einsum("ck,kqs->cqs", basis, coefficients, precision=HIGHEST)
        dual = dual + mask * (local - fitted)
    table_size = directions.shape[1]
    one_hot = (pointing[:, None] == jnp.arange(table_size, dtype=jnp.int32)[None, :]).astype(
        jnp.float32
    )
    pointed = jnp.dot(one_hot, directions.T, precision=HIGHEST)
    projected = pointed[:, 0:1] * positions[0][None, :] + pointed[:, 1:2] * positions[1][None, :]
    ratio = 1.0 + 0.3 * (channel_ids.astype(jnp.float32) + 0.5) / total
    weights = beam_matrices(fitted[0], usable[0], ratio[0], projected)
    samples = voltages.shape[2]
    half = samples // 2
    pieces = []
    for part_index in range(2):
        start = part_index * half
        powers = [detect(weights, voltages[0, :, start : start + half])]
        pieces.append(
            lax.all_to_all(
                average_pairs(jnp.stack(powers, axis=1)),
                "chan",
                split_axis=0,
                concat_axis=1,
                tiled=True,
            )
        )
    beam_power = jnp.concatenate(pieces, axis=2)
    return (beam_power, fitted)


def solution(mesh):
    return jax.shard_map(
        body,
        mesh=mesh,
        in_specs=(
            P(("group", "chan"), None, None, None),
            P(("group", "chan"), None, None),
            P(("group", "chan"), None, None),
            P(("group", "chan"), None),
            P(),
            P(),
            P("group"),
        ),
        out_specs=(P(("group", "chan"), None, None), P(("group", "chan"), None, None)),
        check_vma=False,
    )
```

profile of v0, /device:TPU:0, one launch (start us, length us, event | category | flops | bytes accessed | tf_op | source)
XLA Modules:
  0.0 697.2 jit_solution(10860283058843665609)
XLA Ops:
  7.4 0.7 convert_element_type.35
  8.1 0.7 broadcast_in_dim.6
  8.8 0.7 multiply_bitcast_fusion
  9.5 0.7 multiply_bitcast_fusion.8
  10.4 1.6 broadcast_multiply_fusion.7
  12.1 2.0 fusion
  14.2 94.6 %all-reduce.3.cloned.1.call-done = (f32[4,4,512]{0,1,2:T(4,128)}, f32[4,4,512]{2,1,0:T(4,128)}) async-done(((f32[4,4,512]{0,1,2:T(4,128)}, f32[4,4,512]{2,1,0:T(4,128)}), (f32[4,4,512]{0,1,2:T(4,128)}, f32[4,4,512]{2,1,0:T(4,128)})) %all-reduce.3.cloned.1.call-update) | async-done | bytes 65552 | tf_op jit(solution)/shard_map/psum | solution.py:105
  108.7 0.9 broadcast_add_fusion
  110.4 3.5 convolution_bitcast_fusion.7
  113.9 0.9 fusion.22
  115.7 70.1 %psum.65 = f32[4,4,512]{0,1,2:T(4,128)S(1)} all-reduce(f32[4,4,512]{0,1,2:T(4,128)S(1)} %broadcast_multiply_fusion.6), channel_id=1, replica_groups=mesh['group'=2,'chan'=16] {'chan'}, use_global_device_ids=true, to_apply=%region_2.0 | all-reduce | flops 8192 | bytes 65536 | tf_op jit(solution)/shard_map/psum | solution.py:108
  185.8 3.5 convolution_bitcast_fusion.6
  189.3 0.9 fusion.20
  190.5 0.6 broadcast_multiply_fusion.5
  191.1 69.2 %psum.66 = f32[4,4,512]{0,1,2:T(4,128)S(1)} all-reduce(f32[4,4,512]{0,1,2:T(4,128)S(1)} %broadcast_multiply_fusion.5), channel_id=1, replica_groups=mesh['group'=2,'chan'=16] {'chan'}, use_global_device_ids=true, to_apply=%region_3.0 | all-reduce | flops 8192 | bytes 65536 | tf_op jit(solution)/shard_map/psum | solution.py:108
  260.3 3.5 convolution_bitcast_fusion.5
  263.8 0.9 fusion.18
  265.0 0.6 broadcast_multiply_fusion.4
  265.6 69.4 %psum.67 = f32[4,4,512]{0,1,2:T(4,128)S(1)} all-reduce(f32[4,4,512]{0,1,2:T(4,128)S(1)} %broadcast_multiply_fusion.4), channel_id=1, replica_groups=mesh['group'=2,'chan'=16] {'chan'}, use_global_device_ids=true, to_apply=%region_4.0 | all-reduce | flops 8192 | bytes 65536 | tf_op jit(solution)/shard_map/psum | solution.py:108
  335.0 3.5 convolution_bitcast_fusion.4
  338.5 0.9 fusion.16
  340.3 69.2 %psum.68 = f32[4,4,512]{0,1,2:T(4,128)S(1)} all-reduce(f32[4,4,512]{0,1,2:T(4,128)S(1)} %broadcast_multiply_fusion.3), channel_id=1, replica_groups=mesh['group'=2,'chan'=16] {'chan'}, use_global_device_ids=true, to_apply=%region_5.0 | all-reduce | flops 8192 | bytes 65536 | tf_op jit(solution)/shard_map/psum | solution.py:108
  409.5 3.5 convolution_bitcast_fusion.3
  413.1 0.9 fusion.14
  414.8 69.6 %psum.69 = f32[4,4,512]{0,1,2:T(4,128)S(1)} all-reduce(f32[4,4,512]{0,1,2:T(4,128)S(1)} %broadcast_multiply_fusion.2), channel_id=1, replica_groups=mesh['group'=2,'chan'=16] {'chan'}, use_global_device_ids=true, to_apply=%region_6.0 | all-reduce | flops 8192 | bytes 65536 | tf_op jit(solution)/shard_map/psum | solution.py:108
  484.4 3.5 convolution_bitcast_fusion.2
  487.9 0.9 fusion.12
  489.7 69.2 %psum.70 = f32[4,4,512]{0,1,2:T(4,128)S(1)} all-reduce(f32[4,4,512]{0,1,2:T(4,128)S(1)} %broadcast_multiply_fusion.1), channel_id=1, replica_groups=mesh['group'=2,'chan'=16] {'chan'}, use_global_device_ids=true, to_apply=%region_7.0 | all-reduce | flops 8192 | bytes 65536 | tf_op jit(solution)/shard_map/psum | solution.py:108
  558.9 3.5 convolution_bitcast_fusion.1
  562.4 0.9 fusion.10
  564.2 69.3 %psum.71 = f32[4,4,512]{0,1,2:T(4,128)S(1)} all-reduce(f32[4,4,512]{0,1,2:T(4,128)S(1)} %broadcast_multiply_fusion), channel_id=1, replica_groups=mesh['group'=2,'chan'=16] {'chan'}, use_global_device_ids=true, to_apply=%region_8.0 | all-reduce | flops 8192 | bytes 65536 | tf_op jit(solution)/shard_map/psum | solution.py:108
  633.6 3.5 convolution_bitcast_fusion
  637.1 0.9 fusion.8
  638.1 8.8 %fusion.80 = (bf16[1024,512]{1,0:T(8,128)(2,1)S(1)}, bf16[1024,512]{1,0:T(8,128)(2,1)S(1)}) fusion(f32[512]{0:T(512)S(1)} %bitcast.311, f32[]{:T(128)S(6)} %mul_shard_map.8, f32[512]{0:T(512)S(1)} %bitcast.315, f32[1024]{0:T(1024)S(1)} %bitcast.302, f32[512]{0:T(512)S(1)} %bitcast.313, f32[1024]{0:T(1024)S(1)} %bitcast.300, f32[512]{0:T(512)S(1)} %bitcast.305, ...), kind=kLoop, calls=%fused_computation.196 | loop fusion | flops 10485760 | bytes 2117636 | tf_op jit(solution)/shard_map/neg | solution.py:62
  646.9 9.4 %negate_convert_fusion.1 = (bf16[1024,512]{1,0:T(8,128)(2,1)S(1)}, bf16[1024,512]{1,0:T(8,128)(2,1)S(1)}, bf16[1024,512]{1,0:T(8,128)(2,1)S(1)}, bf16[1024,512]{1,0:T(8,128)(2,1)S(1)}) fusion(f32[]{:T(128)S(6)} %mul_shard_map.8, f32[512]{0:T(512)S(1)} %bitcast.312, f32[512]{0:T(512)S(1)} %bitcast.316, f32[1024]{0:T(1024)S(1)} %bitcast.303, ...), kind=kLoop, calls=%fused_computation.6 | loop fusion | flops 11534336 | bytes 4214788 | tf_op jit(solution)/shard_map/convert_element_type | solution.py:61
  656.3 1.5 fusion.7
  657.8 1.5 fusion.6
  659.3 1.5 fusion.4
  660.8 1.5 fusion.5
  663.3 0.7 reduce.1
  664.2 0.9 reshape.2137
  665.1 3.5 all-to-all-start
  669.2 0.7 reduce
  670.0 0.9 reshape.2135
  670.9 5.6 all-to-all-done
  676.5 3.5 all-to-all-start.1
  681.4 6.4 all-to-all-done.1
  688.8 1.3 copy.102
  (74 shorter events, 9.8 us)
Async XLA Ops:
  7.2 4.9 copy-start
  7.2 101.6 %all-reduce.3.cloned.1.call-start = ((), (), s32[]{:S(2)}) async-start(), calls=%async_computation.2 | async-start | bytes 2162688 | tf_op jit(solution)/shard_map/psum | solution.py:105
  10.3 1.7 copy-start.4
  10.4 1.7 copy-start.6
  108.7 1.6 copy-start.1
  113.9 1.0 copy-start.2
  637.1 1.0 copy-start.3
  646.9 9.4 %copy-start.5 = (bf16[1,2,256,1024]{3,2,1,0:T(8,128)(2,1)S(1)}, bf16[1,2,256,1024]{3,2,1,0:T(8,128)(2,1)}, u32[]{:S(2)}) copy-start(bf16[1,2,256,1024]{3,2,1,0:T(8,128)(2,1)} %param.7) | copy-start | bytes 3145732
  665.1 11.4 %all-to-all-start = ((bf16[16,2,2048]{2,1,0:T(2,128)(2,1)}), bf16[16,2,2048]{2,1,0:T(2,128)(2,1)S(1)}, u32[]{:S(2)}, u32[]{:S(2)}) async-start(bf16[16,2,2048]{2,1,0:T(2,128)(2,1)} %reshape.2137), calls=%async_computation | async-start | bytes 262144 | tf_op jit(solution)/shard_map/all_to_all | solution.py:127
  676.5 11.4 %all-to-all-start.1 = ((bf16[16,2,2048]{2,1,0:T(2,128)(2,1)}), bf16[16,2,2048]{2,1,0:T(2,128)(2,1)S(1)}, u32[]{:S(2)}, u32[]{:S(2)}) async-start(bf16[16,2,2048]{2,1,0:T(2,128)(2,1)} %reshape.2135), calls=%async_computation.1 | async-start | bytes 262144 | tf_op jit(solution)/shard_map/all_to_all | solution.py:127
Sparse Core Ops, SparseCore 0:
  12.1 96.5 all-reduce.2
where the time goes:
time: 704 us; the launch traced here: 697 us
  blocking collectives  486 us (69%)
  waiting for transfers between devices  107 us (15%)
  matrix products  43.8 us (6%)
  other arithmetic  29.8 us (4%)
  between operations  15 us (2%)
  local copies, waits for them, and re-layouts  9.1 us (1%)
  starting transfers between devices  7.06 us (1%)
    psum x7, blocking collectives, body(): summed = lax.psum(numerator, 'chan')  486 us
    psum x1, waiting for transfers between devices, body(): gram_all, summed = lax.psum((gram, numerator), 'chan')  94.6 us
    dot_general x8, matrix products, body(): jnp.einsum('kjs,jqs->kqs', inverse, summed, precision=HIGHEST)  28.4 us
  transfers between devices with their start and end apart: 3, of which 3 were waited for; matrix products, arithmetic and copies ran while one was open for 1% of the time, Pallas kernels for 0%

commit v1 on v0

--- a/solution.py
+++ b/solution.py
@@ -105,7 +105,7 @@
             gram_all, summed = lax.psum((gram, numerator), "chan")
             inverse = invert_small(gram_all + RIDGE * identity)
         else:
-            summed = lax.psum(numerator, "chan")
+            summed = jnp.sum(lax.all_gather(numerator, "chan"), axis=0)
         coefficients = jnp.einsum("kjs,jqs->kqs", inverse, summed, precision=HIGHEST)
         fitted = jnp.einsum("ck,kqs->cqs", basis, coefficients, precision=HIGHEST)
         dual = dual + mask * (local - fitted)

time: 704 us -> 350 us (0.50)
  blocking collectives: 486 us -> 142 us
  waiting for transfers between devices: 107 us -> 98.8 us
    psum x7 -> x0, blocking collectives: 486 us -> none  [body(): summed = lax.psum(numerator, 'chan')]
    all_gather x0 -> x7, blocking collectives: none -> 142 us  [body(): summed = jnp.sum(lax.all_gather(numerator, 'chan'), axis=0)]
    psum x1, waiting for transfers between devices: 94.6 us -> 86.8 us  [body(): gram_all, summed = lax.psum((gram, numerator), 'chan')]
  transfers between devices with their start and end apart: 3 -> 3, of which waited for: 3 -> 3; matrix products, arithmetic and copies ran while one was open for 1% -> 2% of each run, Pallas kernels for 0% -> 0%
where the time goes in v1:
time: 350 us; the launch traced here: 344 us
  blocking collectives  142 us (41%)
  waiting for transfers between devices  98.8 us (28%)
  matrix products  44.5 us (13%)
  other arithmetic  25.6 us (7%)
  between operations  14.8 us (4%)
  local copies, waits for them, and re-layouts  12 us (3%)
  starting transfers between devices  7.06 us (2%)
    all_gather x7, blocking collectives, body(): summed = jnp.sum(lax.all_gather(numerator, 'chan'), axis=0)  142 us
    psum x1, waiting for transfers between devices, body(): gram_all, summed = lax.psum((gram, numerator), 'chan')  86.8 us
    dot_general x8, matrix products, body(): jnp.einsum('kjs,jqs->kqs', inverse, summed, precision=HIGHEST)  28.4 us
    all_to_all x2, waiting for transfers between devices, body(): lax.all_to_all(average_pairs(jnp.stack(powers, axis=1)), 'chan', split_ax...  12 us
    convert_element_type x1, other arithmetic, beam_matrices(): w_im = (-(gain_re * sine + gain_im * cosine)).astype(jnp.bfloat16)  9.18 us
    neg x1, other arithmetic, beam_matrices(): upper = jnp.concatenate([w_re, -w_im], axis=1)  8.97 us
    dot_general x8, matrix products, body(): fitted = jnp.einsum('ck,kqs->cqs', basis, coefficients, precision=HIGHEST)  7.55 us
    all_to_all x2, starting transfers between devices, body(): lax.all_to_all(average_pairs(jnp.stack(powers, axis=1)), 'chan', split_ax...  7.02 us
  transfers between devices with their start and end apart: 3, of which 3 were waited for; matrix products, arithmetic and copies ran while one was open for 2% of the time, Pallas kernels for 0%

profile of v1, /device:TPU:0, one launch (start us, length us, event | category | flops | bytes accessed | tf_op | source)
XLA Modules:
  0.0 344.4 jit_solution(4167736684230929887)
XLA Ops:
  7.4 0.7 convert_element_type.35
  8.1 0.7 broadcast_in_dim.6
  8.8 0.7 multiply_bitcast_fusion.8
  9.5 0.7 broadcast_multiply_fusion.7
  10.2 0.7 multiply_bitcast_fusion
  10.9 0.8 fusion.94
  11.7 2.7 fusion
  14.5 86.8 %all-reduce.3.cloned.1.call-done = (f32[4,4,512]{2,1,0:T(4,128)}, f32[4,4,512]{2,1,0:T(4,128)}) async-done(((f32[4,4,512]{2,1,0:T(4,128)}, f32[4,4,512]{2,1,0:T(4,128)}), (f32[4,4,512]{2,1,0:T(4,128)}, f32[4,4,512]{2,1,0:T(4,128)})) %all-reduce.3.cloned.1.call-update) | async-done | bytes 65552 | tf_op jit(solution)/shard_map/psum | solution.py:105
  101.2 0.8 broadcast_add_fusion
  103.2 3.5 %convolution_bitcast_fusion.7 = f32[4,4,512]{0,1,2:T(4,128)S(1)} fusion(f32[4,4,512]{0,1,2:T(4,128)S(1)} %copy.131, f32[4,4,512]{1,0,2:T(4,128)S(1)} %copy.132), kind=kOutput, calls=%fused_computation.19 | convolution fusion | flops 393216 | bytes 98304 | tf_op jit(solution)/shard_map/kjs,jqs->kqs/dot_general | solution.py:109
  106.8 0.9 fusion.22
  107.8 23.6 %all-gather = f32[64,4,512]{2,1,0:T(4,128)S(1)} all-gather(f32[4,4,512]{2,1,0:T(4,128)S(1)} %broadcast_multiply_fusion.6), channel_id=2, replica_groups=mesh['group'=2,'chan'=16] {'chan'}, dimensions={0}, use_global_device_ids=true | all-gather | bytes 557056 | tf_op jit(solution)/shard_map/all_gather | solution.py:108
  132.0 3.5 %convolution_bitcast_fusion.6 = f32[4,4,512]{0,1,2:T(4,128)S(1)} fusion(f32[4,4,512]{0,1,2:T(4,128)S(1)} %copy.133, f32[4,4,512]{1,0,2:T(4,128)S(1)} %copy.132), kind=kOutput, calls=%fused_computation.18 | convolution fusion | flops 393216 | bytes 98304 | tf_op jit(solution)/shard_map/kjs,jqs->kqs/dot_general | solution.py:109
  135.5 0.9 fusion.20
  136.6 18.9 %all-gather.1 = f32[64,4,512]{2,1,0:T(4,128)S(1)} all-gather(f32[4,4,512]{2,1,0:T(4,128)S(1)} %broadcast_multiply_fusion.5), channel_id=3, replica_groups=mesh['group'=2,'chan'=16] {'chan'}, dimensions={0}, use_global_device_ids=true | all-gather | bytes 557056 | tf_op jit(solution)/shard_map/all_gather | solution.py:108
  156.0 3.5 %convolution_bitcast_fusion.5 = f32[4,4,512]{0,1,2:T(4,128)S(1)} fusion(f32[4,4,512]{0,1,2:T(4,128)S(1)} %copy.135, f32[4,4,512]{1,0,2:T(4,128)S(1)} %copy.132), kind=kOutput, calls=%fused_computation.17 | convolution fusion | flops 393216 | bytes 98304 | tf_op jit(solution)/shard_map/kjs,jqs->kqs/dot_general | solution.py:109
  159.5 0.9 fusion.18
  160.6 20.5 %all-gather.2 = f32[64,4,512]{2,1,0:T(4,128)S(1)} all-gather(f32[4,4,512]{2,1,0:T(4,128)S(1)} %broadcast_multiply_fusion.4), channel_id=4, replica_groups=mesh['group'=2,'chan'=16] {'chan'}, dimensions={0}, use_global_device_ids=true | all-gather | bytes 557056 | tf_op jit(solution)/shard_map/all_gather | solution.py:108
  181.6 3.5 %convolution_bitcast_fusion.4 = f32[4,4,512]{0,1,2:T(4,128)S(1)} fusion(f32[4,4,512]{0,1,2:T(4,128)S(1)} %copy.137, f32[4,4,512]{1,0,2:T(4,128)S(1)} %copy.132), kind=kOutput, calls=%fused_computation.16 | convolution fusion | flops 393216 | bytes 98304 | tf_op jit(solution)/shard_map/kjs,jqs->kqs/dot_general | solution.py:109
  185.2 0.9 fusion.16
  186.3 18.9 %all-gather.3 = f32[64,4,512]{2,1,0:T(4,128)S(1)} all-gather(f32[4,4,512]{2,1,0:T(4,128)S(1)} %broadcast_multiply_fusion.3), channel_id=5, replica_groups=mesh['group'=2,'chan'=16] {'chan'}, dimensions={0}, use_global_device_ids=true | all-gather | bytes 557056 | tf_op jit(solution)/shard_map/all_gather | solution.py:108
  205.6 3.5 %convolution_bitcast_fusion.3 = f32[4,4,512]{0,1,2:T(4,128)S(1)} fusion(f32[4,4,512]{0,1,2:T(4,128)S(1)} %copy.139, f32[4,4,512]{1,0,2:T(4,128)S(1)} %copy.132), kind=kOutput, calls=%fused_computation.15 | convolution fusion | flops 393216 | bytes 98304 | tf_op jit(solution)/shard_map/kjs,jqs->kqs/dot_general | solution.py:109
  209.2 0.9 fusion.14
  210.3 20.7 %all-gather.4 = f32[64,4,512]{2,1,0:T(4,128)S(1)} all-gather(f32[4,4,512]{2,1,0:T(4,128)S(1)} %broadcast_multiply_fusion.2), channel_id=6, replica_groups=mesh['group'=2,'chan'=16] {'chan'}, dimensions={0}, use_global_device_ids=true | all-gather | bytes 557056 | tf_op jit(solution)/shard_map/all_gather | solution.py:108
  231.5 3.5 %convolution_bitcast_fusion.2 = f32[4,4,512]{0,1,2:T(4,128)S(1)} fusion(f32[4,4,512]{0,1,2:T(4,128)S(1)} %copy.141, f32[4,4,512]{1,0,2:T(4,128)S(1)} %copy.132), kind=kOutput, calls=%fused_computation.14 | convolution fusion | flops 393216 | bytes 98304 | tf_op jit(solution)/shard_map/kjs,jqs->kqs/dot_general | solution.py:109
  235.0 0.9 fusion.12
  236.1 18.9 %all-gather.5 = f32[64,4,512]{2,1,0:T(4,128)S(1)} all-gather(f32[4,4,512]{2,1,0:T(4,128)S(1)} %broadcast_multiply_fusion.1), channel_id=7, replica_groups=mesh['group'=2,'chan'=16] {'chan'}, dimensions={0}, use_global_device_ids=true | all-gather | bytes 557056 | tf_op jit(solution)/shard_map/all_gather | solution.py:108
  255.5 3.5 %convolution_bitcast_fusion.1 = f32[4,4,512]{0,1,2:T(4,128)S(1)} fusion(f32[4,4,512]{0,1,2:T(4,128)S(1)} %copy.143, f32[4,4,512]{1,0,2:T(4,128)S(1)} %copy.132), kind=kOutput, calls=%fused_computation.13 | convolution fusion | flops 393216 | bytes 98304 | tf_op jit(solution)/shard_map/kjs,jqs->kqs/dot_general | solution.py:109
  259.0 0.9 fusion.10
  260.1 20.3 %all-gather.6 = f32[64,4,512]{2,1,0:T(4,128)S(1)} all-gather(f32[4,4,512]{2,1,0:T(4,128)S(1)} %broadcast_multiply_fusion), channel_id=8, replica_groups=mesh['group'=2,'chan'=16] {'chan'}, dimensions={0}, use_global_device_ids=true | all-gather | bytes 557056 | tf_op jit(solution)/shard_map/all_gather | solution.py:108
  280.9 3.5 %convolution_bitcast_fusion = f32[4,4,512]{0,1,2:T(4,128)S(1)} fusion(f32[4,4,512]{0,1,2:T(4,128)S(1)} %copy.145, f32[4,4,512]{1,0,2:T(4,128)S(1)} %copy.132), kind=kOutput, calls=%fused_computation.12 | convolution fusion | flops 393216 | bytes 98304 | tf_op jit(solution)/shard_map/kjs,jqs->kqs/dot_general | solution.py:109
  284.5 0.9 fusion.8
  285.5 9.0 %fusion.80 = (bf16[1024,512]{1,0:T(8,128)(2,1)S(1)}, bf16[1024,512]{1,0:T(8,128)(2,1)S(1)}) fusion(f32[512]{0:T(512)S(1)} %bitcast.325, f32[]{:T(128)S(6)} %mul_shard_map.8, f32[512]{0:T(512)S(1)} %bitcast.329, f32[1024]{0:T(1024)S(1)} %bitcast.316, f32[512]{0:T(512)S(1)} %bitcast.327, f32[1024]{0:T(1024)S(1)} %bitcast.314, f32[512]{0:T(512)S(1)} %bitcast.319, ...), kind=kLoop, calls=%fused_computation.196 | loop fusion | flops 10485760 | bytes 2117636 | tf_op jit(solution)/shard_map/neg | solution.py:62
  294.4 9.2 %negate_convert_fusion.1 = (bf16[1024,512]{1,0:T(8,128)(2,1)S(1)}, bf16[1024,512]{1,0:T(8,128)(2,1)S(1)}, bf16[1024,512]{1,0:T(8,128)(2,1)S(1)}, bf16[1024,512]{1,0:T(8,128)(2,1)S(1)}) fusion(f32[]{:T(128)S(6)} %mul_shard_map.8, f32[512]{0:T(512)S(1)} %bitcast.326, f32[512]{0:T(512)S(1)} %bitcast.330, f32[1024]{0:T(1024)S(1)} %bitcast.317, ...), kind=kLoop, calls=%fused_computation.6 | loop fusion | flops 11534336 | bytes 4214788 | tf_op jit(solution)/shard_map/convert_element_type | solution.py:61
  303.6 1.5 fusion.7
  305.1 1.5 fusion.6
  306.6 1.5 fusion.4
  308.1 1.5 fusion.5
  310.6 0.7 reduce.1
  311.5 0.9 reshape.2144
  312.4 3.5 %all-to-all-start = ((bf16[16,2,2048]{2,1,0:T(2,128)(2,1)}), bf16[16,2,2048]{2,1,0:T(2,128)(2,1)S(1)}, u32[]{:S(2)}, u32[]{:S(2)}) async-start(bf16[16,2,2048]{2,1,0:T(2,128)(2,1)} %reshape.2144), calls=%async_computation | async-start | bytes 262144 | tf_op jit(solution)/shard_map/all_to_all | solution.py:127
  316.4 0.7 reduce
  317.3 0.9 reshape.2142
  318.2 5.6 %all-to-all-done = bf16[16,2,2048]{2,1,0:T(2,128)(2,1)S(1)} async-done(((bf16[16,2,2048]{2,1,0:T(2,128)(2,1)}), bf16[16,2,2048]{2,1,0:T(2,128)(2,1)S(1)}, u32[]{:S(2)}, u32[]{:S(2)}) %all-to-all-start) | async-done | bytes 131104 | tf_op jit(solution)/shard_map/all_to_all | solution.py:127
  323.7 3.5 %all-to-all-start.1 = ((bf16[16,2,2048]{2,1,0:T(2,128)(2,1)}), bf16[16,2,2048]{2,1,0:T(2,128)(2,1)S(1)}, u32[]{:S(2)}, u32[]{:S(2)}) async-start(bf16[16,2,2048]{2,1,0:T(2,128)(2,1)} %reshape.2142), calls=%async_computation.1 | async-start | bytes 262144 | tf_op jit(solution)/shard_map/all_to_all | solution.py:127
  327.3 0.6 copy.167
  328.7 6.4 %all-to-all-done.1 = bf16[16,2,2048]{2,1,0:T(2,128)(2,1)S(1)} async-done(((bf16[16,2,2048]{2,1,0:T(2,128)(2,1)}), bf16[16,2,2048]{2,1,0:T(2,128)(2,1)S(1)}, u32[]{:S(2)}, u32[]{:S(2)}) %all-to-all-start.1) | async-done | bytes 131104 | tf_op jit(solution)/shard_map/all_to_all | solution.py:127
  336.1 1.3 copy.151
  (77 shorter events, 9.5 us)
Async XLA Ops:
  7.2 4.5 %copy-start = (f32[2,1024]{1,0:T(2,128)S(1)}, f32[2,1024]{1,0:T(2,128)}, u32[]{:S(2)}) copy-start(f32[2,1024]{1,0:T(2,128)} %param.12) | copy-start | bytes 24580
  7.2 94.0 %all-reduce.3.cloned.1.call-start = ((), (), s32[]{:S(2)}) async-start(), calls=%async_computation.2 | async-start | bytes 131072 | tf_op jit(solution)/shard_map/psum | solution.py:105
  101.2 1.6 copy-start.2
  106.8 1.0 copy-start.1
  284.5 1.0 copy-start.3
  294.4 9.2 %copy-start.4 = (bf16[1,2,256,1024]{3,2,1,0:T(8,128)(2,1)S(1)}, bf16[1,2,256,1024]{3,2,1,0:T(8,128)(2,1)}, u32[]{:S(2)}) copy-start(bf16[1,2,256,1024]{3,2,1,0:T(8,128)(2,1)} %param.7) | copy-start | bytes 3145732
  312.4 11.4 %all-to-all-start = ((bf16[16,2,2048]{2,1,0:T(2,128)(2,1)}), bf16[16,2,2048]{2,1,0:T(2,128)(2,1)S(1)}, u32[]{:S(2)}, u32[]{:S(2)}) async-start(bf16[16,2,2048]{2,1,0:T(2,128)(2,1)} %reshape.2144), calls=%async_computation | async-start | bytes 262144 | tf_op jit(solution)/shard_map/all_to_all | solution.py:127
  323.7 11.4 %all-to-all-start.1 = ((bf16[16,2,2048]{2,1,0:T(2,128)(2,1)}), bf16[16,2,2048]{2,1,0:T(2,128)(2,1)S(1)}, u32[]{:S(2)}, u32[]{:S(2)}) async-start(bf16[16,2,2048]{2,1,0:T(2,128)(2,1)} %reshape.2142), calls=%async_computation.1 | async-start | bytes 262144 | tf_op jit(solution)/shard_map/all_to_all | solution.py:127
Sparse Core Ops, SparseCore 0:
  12.1 89.0 all-reduce.2
